TPU v7x, 32 devices: a whole 2x2x4 slice. The times are simulated.
32 devices in a mesh: seg: 4 (over y, core), sec: 8 (over z, x).
Axes of the slice: x: 2, y: 2, z: 4, core: 2. Of those that a mesh axis runs over, the one named last changes fastest.
Arguments:
- left_env: bfloat16 [4, 8, 3, 512, 512], P('seg', 'sec'), may hold values from -0.25 to 0.25
- right_env: bfloat16 [4, 8, 3, 512, 512], P('seg', 'sec'), may hold values from -0.25 to 0.25
- psi: bfloat16 [4, 8, 512, 512], P('seg', 'sec'), may hold values from -6 to 6
- orders: int32 [4, 8, 2], P('seg', 'sec'), may hold values from 64 to 512, as said below
- sources: int32 [3, 8], replicated, may hold values from 0 to 7, each once within a row
- active: int32 [4, 8, 3], P('seg', 'sec'), may hold values 0 or 1
Outputs:
- applied: bfloat16 [4, 8, 512, 512], P('seg', 'sec')
Inputs may be any that keep to these rules, and one draw needn't show every extreme that they name: In every bond one sector has both orders equal to 512. `sources`: each row is a permutation of the sectors.
All inputs are finite; a program needn't handle non-finite values. No bound on the sum of `active` on one device may be relied on, other than what follows from the above.
Results may differ from a plain program's by a relative error of at most 0.008.
Values may be sent and summed in bfloat16 or wider, within the bound.
No kernel may reach another device: no remote copies, remote signals or barrier semaphores. Data moves between devices by JAX's collectives and lax.ppermute only.
A program may use at most 64 MiB of HBM per device.

v0:
```python
import jax
import jax.numpy as jnp
from jax import lax
from jax.sharding import PartitionSpec as P


def passed_along(block, axis, distance):
    devices = range(lax.axis_size(axis))
    route = [((i - distance) % len(devices), i) for i in devices]
    return lax.ppermute(block, axis, route)


def sector_masks(order_rows, padded):
    positions = jnp.arange(padded, dtype=jnp.int32)
    upper = positions[None, :, None] < order_rows[:, 0][:, None, None]
    lower = positions[None, None, :] < order_rows[:, 1][:, None, None]
    return upper & lower


def body(left_env, right_env, psi, orders, sources, active):
    padded = psi.shape[-1]
    per_dev = psi.shape[1]
    shifted = passed_along(right_env, "seg", -1)
    inside_mask = sector_masks(orders[0], padded)
    masked_psi = jnp.where(inside_mask, psi[0], jnp.zeros((), psi.dtype))
    own_start = lax.axis_index("sec") * per_dev
    wanted = lax.dynamic_slice_in_dim(sources, own_start, per_dev, 1).T
    empty_blocks = jnp.zeros((per_dev, wanted.shape[1], padded, padded), psi.dtype)
    piece = lax.all_gather(masked_psi, "sec", axis=0, tiled=True)
    piece_rows = piece.shape[0]
    inside = (wanted >= 0) & (wanted < piece_rows)
    chosen = piece[jnp.clip(wanted, 0, piece_rows - 1)]
    picked = jnp.where(inside[:, :, None, None], chosen, empty_blocks)
    left_product = jnp.einsum(
        "swab,swbc->swac", left_env[0], picked, preferred_element_type=jnp.float32
    ).astype(jnp.bfloat16)
    full_product = jnp.einsum(
        "swac,swdc->swad", left_product, shifted[0], preferred_element_type=jnp.float32
    )
    weights = active[0].astype(jnp.float32)
    summed = jnp.sum(full_product * weights[:, :, None, None], axis=1)
    return jnp.where(inside_mask, summed, 0.0).astype(jnp.bfloat16)[None]


def solution(mesh):
    placed = (
        P("seg", "sec", None, None, None),
        P("seg", "sec", None, None, None),
        P("seg", "sec", None, None),
        P("seg", "sec", None),
        P(),
        P("seg", "sec", None),
    )
    return jax.shard_map(
        body, mesh=mesh, in_specs=placed, out_specs=P("seg", "sec", None, None), check_vma=False
    )
```

profile of v0, /device:TPU:0, one launch (start us, length us, event | category | flops | bytes accessed | tf_op | source)
XLA Modules:
  0.0 102.8 jit_solution(14573823378877413567)
XLA Ops:
  6.5 0.0 copy-start
  6.5 0.0 copy-start.1
  6.5 0.0 copy-start.2
  6.5 0.0 all-gather.2.cloned.1.call-start
  6.5 1.4 %fusion.14 = (s32[1,1]{1,0:T(1,128)}, s32[1,1]{1,0:T(1,128)}) fusion(s32[1,2]{1,0:T(1,128)} %bitcast.23), kind=kLoop, calls=%fused_computation.20 | loop fusion | bytes 16 | tf_op jit(solution)/shard_map/slice | solution.py:15
  7.9 1.2 %iota_compare_fusion = (pred[512]{0:T(512)(128)(4,1)S(1)}, pred[512]{0:T(512)(128)(4,1)S(1)}) fusion(s32[]{:T(128)} %bitcast.2, s32[]{:T(128)} %bitcast.1), kind=kLoop, calls=%fused_computation.14 | loop fusion | flops 1024 | bytes 1032 | tf_op jit(solution)/shard_map/lt | solution.py:16
  9.1 2.1 %and_select_fusion = bf16[1,512,512]{2,1,0:T(8,128)(2,1)} fusion(bf16[1,1,512,512]{3,2,1,0:T(8,128)(2,1)} %param.8, pred[512]{0:T(512)(128)(4,1)S(1)} %get-tuple-element.7, pred[512]{0:T(512)(128)(4,1)S(1)} %get-tuple-element.8), kind=kLoop, calls=%fused_computation.9 | loop fusion | flops 524288 | bytes 1049600 | tf_op jit(solution)/shard_map/jit(_where)/select_n | solution.py:25
  11.2 0.0 all-gather.2.cloned.1.call-update
  11.2 2.5 %collective-permute-start = (bf16[1,1,3,512,512]{4,3,2,1,0:T(8,128)(2,1)}, bf16[1,1,3,512,512]{4,3,2,1,0:T(8,128)(2,1)}, u32[]{:S(2)}, u32[]{:S(2)}) collective-permute-start(bf16[1,1,3,512,512]{4,3,2,1,0:T(8,128)(2,1)} %param.7), channel_id=1, source_target_pairs={{8,0},{16,8},{24,16},{0,24},{9,1},{17,9},{25,17},{1,25},{10,2},{18... | collective-permute-start | bytes 4718600 | tf_op jit(solution)/shard_map/ppermute | solution.py:10
  13.7 0.0 copy-done.1
  13.7 0.2 clamp_reduce_fusion
  13.9 0.2 and_reduce_fusion
  14.1 0.0 copy-done.2
  14.1 72.8 %all-gather.2.cloned.1.call-done = bf16[8,512,512]{2,1,0:T(8,128)(2,1)} async-done(((bf16[1,512,512]{2,1,0:T(8,128)(2,1)}), bf16[8,512,512]{2,1,0:T(8,128)(2,1)}) %all-gather.2.cloned.1.call-update) | async-done | bytes 4194320 | tf_op jit(solution)/shard_map/all_gather | solution.py:29
  86.9 2.8 %gather_fusion = bf16[3,512,512]{2,1,0:T(8,128)(2,1)S(1)} fusion(bf16[8,512,512]{2,1,0:T(8,128)(2,1)} %all-gather.2.cloned.1.call-done, s32[1024]{0:T(1024)S(1)} %pad_clamp_fusion), kind=kCustom, calls=%fused_computation | custom fusion | bytes 3145740 | tf_op jit(solution)/shard_map/gather | solution.py:32
  89.7 0.0 collective-permute-done
  89.7 0.0 copy-done
  89.7 4.2 %multiply_reduce_fusion = bf16[512,512]{1,0:T(8,128)(2,1)} fusion(bf16[1,1,3,512,512]{4,3,2,1,0:T(8,128)(2,1)} %collective-permute-done, f32[3]{0:T(128)S(1)} %convert_bitcast_fusion, bf16[1,1,3,512,512]{4,3,2,1,0:T(8,128)(2,1)S(1)} %copy-done, bf16[3,512,512]{2,1,0:T(8,128)(2,1)S(1)} %gather_fusion, pred[3]{0:T(512)(128)(4,1)S(1)} %and_reduce_fusion), kind=kOutput, calls=%fused_computation.1 | convolution fusion | flops 1613496320 | bytes 5242895 | tf_op jit(solution)/shard_map/swac,swdc->swad/dot_general | solution.py:37
  93.9 2.1 %fusion.4 = bf16[1,1,512,512]{3,2,1,0:T(8,128)(2,1)} fusion(bf16[512,512]{1,0:T(8,128)(2,1)} %multiply_reduce_fusion, pred[512]{0:T(512)(128)(4,1)S(1)} %get-tuple-element.7, pred[512]{0:T(512)(128)(4,1)S(1)} %get-tuple-element.8), kind=kLoop, calls=%fused_computation.8 | loop fusion | flops 524288 | bytes 1049600 | tf_op jit(solution)/shard_map/convert_element_type | solution.py:42
  (3 shorter events, 0.0 us)
Async XLA Ops:
  6.5 83.2 %copy-start = (bf16[1,1,3,512,512]{4,3,2,1,0:T(8,128)(2,1)S(1)}, bf16[1,1,3,512,512]{4,3,2,1,0:T(8,128)(2,1)}, u32[]{:S(2)}) copy-start(bf16[1,1,3,512,512]{4,3,2,1,0:T(8,128)(2,1)} %param.6) | copy-start | bytes 4718596
  6.5 7.2 %copy-start.1 = (s32[3,8]{1,0:T(4,128)S(1)}, s32[3,8]{1,0:T(4,128)}, u32[]{:S(2)}) copy-start(s32[3,8]{1,0:T(4,128)} %param.10) | copy-start | bytes 292
  6.5 7.6 %copy-start.2 = (s32[1,1,3]{2,1,0:T(1,128)S(1)}, s32[1,1,3]{2,1,0:T(1,128)}, u32[]{:S(2)}) copy-start(s32[1,1,3]{2,1,0:T(1,128)} %param.11) | copy-start | bytes 40
  6.5 80.3 %all-gather.2.cloned.1.call-start = ((), (), s32[]{:S(2)}) async-start(), calls=%async_computation | async-start | bytes 4718592 | tf_op jit(solution)/shard_map/all_gather | solution.py:29
  11.2 78.5 %collective-permute-start = (bf16[1,1,3,512,512]{4,3,2,1,0:T(8,128)(2,1)}, bf16[1,1,3,512,512]{4,3,2,1,0:T(8,128)(2,1)}, u32[]{:S(2)}, u32[]{:S(2)}) collective-permute-start(bf16[1,1,3,512,512]{4,3,2,1,0:T(8,128)(2,1)} %param.7), channel_id=1, source_target_pairs={{8,0},{16,8},{24,16},{0,24},{9,1},{17,9},{25,17},{1,25},{10,2},{18... | collective-permute-start | bytes 4718600 | tf_op jit(solution)/shard_map/ppermute | solution.py:10
Sparse Core Ops, SparseCore 0:
  11.3 75.4 all-gather.1
where the time goes:
time: 103 us
  waiting for transfers between devices  72.8 us (71%)
  between operations  13.5 us (13%)
  other arithmetic  5.71 us (6%)
  local copies, waits for them, and re-layouts  4.21 us (4%)
  matrix products  4.19 us (4%)
  starting transfers between devices  2.49 us (2%)
    all_gather x1, waiting for transfers between devices, body(): piece = lax.all_gather(masked_psi, 'sec', axis=0, tiled=True)  72.8 us
    dot_general x1, matrix products, body(): jnp.einsum('swac,swdc->swad', left_product, shifted[0], preferred_element...  4.19 us
    gather x1, local copies, waits for them, and re-layouts, body(): chosen = piece[jnp.clip(wanted, 0, piece_rows - 1)]  2.83 us
    ppermute x1, starting transfers between devices, passed_along(): return lax.ppermute(block, axis, route)  2.49 us
  transfers between devices with their start and end apart: 2, of which 1 were waited for; matrix products, arithmetic and copies ran while one was open for 3% of the time, Pallas kernels for 0%

commit v1 on v0

v1 whole, which is shorter than its diff:
```python
import functools

import jax
import jax.numpy as jnp
from jax import lax
from jax.experimental import pallas as pl
from jax.experimental.pallas import tpu as pltpu
from jax.sharding import PartitionSpec as P


PAIR = 2


def place_in_ring(plane, planes):
    return jnp.where(plane % 2 == 1, (plane + 1) // 2, (planes - plane // 2) % planes)


def ring_route(planes):
    ring = [0, *range(1, planes, 2), *reversed(range(2, planes, 2))]
    steps = zip(ring, ring[1:] + ring[:1])
    return [(a * PAIR + c, b * PAIR + c) for a, b in steps for c in range(PAIR)]


def held_as(sector, holder, planes):
    at = place_in_ring(holder // PAIR, planes)
    of = place_in_ring(sector // PAIR, planes)
    return PAIR * lax.rem(at - of + planes, planes) + lax.rem(sector + holder, PAIR)


def slots_of(keys, last):
    slots = []
    for mine in keys:
        later = 0
        for i, other in enumerate(keys):
            fresh = (other > mine) & (other < last)
            for before in keys[:i]:
                fresh = fresh & (before != other)
            later = later + fresh.astype(jnp.int32)
        slots.append(jnp.where(mine == last, len(keys), len(keys) - 1 - later))
    return slots


class Plan:
    def __init__(self, terms):
        self.send, self.own, self.slot, self.active = 0, terms, 2 * terms, 3 * terms
        self.order = 4 * terms
        self.rows = 4 * terms + 2

    @staticmethod
    def read(ref, row):
        return jnp.max(ref[pl.ds(row, 1), :])


def fetch(pairs, sem):
    copies = [pltpu.make_async_copy(*pair, sem.at[i]) for i, pair in enumerate(pairs)]
    for copy in copies:
        copy.start()
    for copy in copies:
        copy.wait()


def plan_kernel(planes, sources_hbm, active_hbm, orders_hbm, out_ref, sources_ref, active_ref, orders_ref, sem):
    fetch([(sources_hbm, sources_ref), (active_hbm, active_ref), (orders_hbm, orders_ref)], sem)
    terms = sources_ref.shape[0]
    plan = Plan(terms)
    me = lax.axis_index("sec")
    partner = me + 1 - PAIR * lax.rem(me, PAIR)
    last = PAIR * planes - 1

    def put(row, value):
        out_ref[pl.ds(row, 1), :] = jnp.full((1, out_ref.shape[1]), value, jnp.int32)

    keys = [held_as(sources_ref[w, partner], me, planes) for w in range(terms)]
    slots = slots_of(keys, last)
    for slot in range(terms):
        wanted = jnp.int32(0)
        for key, at in zip(keys, slots):
            wanted = jnp.where(at == slot, key, wanted)
        put(plan.send + slot, wanted)
    wanted = [sources_ref[w, me] for w in range(terms)]
    slots = slots_of([held_as(s, partner, planes) for s in wanted], last)
    for w in range(terms):
        put(plan.own + w, held_as(wanted[w], me, planes))
        put(plan.slot + w, slots[w])
        put(plan.active + w, active_ref[0, 0, w])
    for side in range(2):
        put(plan.order + side, orders_ref[0, 0, side])


def split_kernel(orders_hbm, psi_hbm, mine_ref, other_ref, orders_ref, psi_ref, sem):
    fetch([(psi_hbm, psi_ref), (orders_hbm, orders_ref)], sem)
    rows, width = mine_ref.shape
    side = lax.rem(lax.axis_index("sec"), PAIR)
    row = lax.broadcasted_iota(jnp.int32, (rows, width), 0)
    column = lax.broadcasted_iota(jnp.int32, (rows, width), 1)
    for ref, half in ((other_ref, PAIR - 1 - side), (mine_ref, side)):
        start = pl.multiple_of(half * width, width)
        inside = (row < orders_ref[0, 0, 0]) & (column + start < orders_ref[0, 0, 1])
        values = psi_ref[0, 0, :, pl.ds(start, width)]
        ref[...] = jnp.where(inside, values, jnp.zeros((), values.dtype))


def choose_kernel(row, plan_ref, *refs):
    *held, out_ref = refs
    wanted = Plan.read(plan_ref, row)
    for i, ref in enumerate(held):

        @pl.when(wanted == i)
        def _(ref=ref):
            out_ref[...] = ref[...]


def apply_kernel(terms, owned, slotted, first, final, plan_ref, left_ref, right_ref, *refs):
    plan = Plan(terms)
    held, refs = refs[: len(owned)], refs[len(owned) :]
    passed, refs = refs[: len(slotted)], refs[len(slotted) :]
    if first:
        out_ref, blocks = refs
        total = out_ref
        total[...] = jnp.zeros_like(total)
    else:
        before_ref, out_ref, blocks, total = refs if final else (*refs, refs[1])
        total[...] = before_ref[...]
    width = blocks.shape[-1]
    side = lax.rem(lax.axis_index("sec"), PAIR)
    for w in range(terms):
        active = Plan.read(plan_ref, plan.active + w) != 0
        for kind, row, places, arrived in ((0, plan.own, owned, held), (1, plan.slot, slotted, passed)):
            if not places:
                continue
            at = Plan.read(plan_ref, row + w)
            for place, ref in zip(places, arrived):

                @pl.when(at == place)
                def _(ref=ref):
                    blocks[...] = ref[...]

            @pl.when(active & (at >= places[0]) & (at <= places[-1]))
            def _():
                half = side if kind == 0 else PAIR - 1 - side
                start = pl.multiple_of(half * width, width)
                product = jnp.dot(left_ref[0, 0, w], blocks[...], preferred_element_type=jnp.float32)
                total[...] += lax.dot_general(
                    product.astype(blocks.dtype),
                    right_ref[0, 0, w, :, pl.ds(start, width)],
                    (((1,), (1,)), ((), ())),
                    preferred_element_type=jnp.float32,
                )

    if final:
        row = lax.broadcasted_iota(jnp.int32, total.shape, 0)
        column = lax.broadcasted_iota(jnp.int32, total.shape, 1)
        inside = (row < Plan.read(plan_ref, plan.order)) & (column < Plan.read(plan_ref, plan.order + 1))
        out_ref[0, 0] = jnp.where(inside, total[...], 0.0).astype(out_ref.dtype)


ROOM = pltpu.CompilerParams(vmem_limit_bytes=24 << 20)
HBM = pl.BlockSpec(memory_space=pltpu.HBM)
VMEM = pl.BlockSpec(memory_space=pltpu.VMEM)


def near(array):
    return pltpu.with_memory_space_constraint(array, pltpu.VMEM)


def far(array):
    return pltpu.with_memory_space_constraint(array, pltpu.HBM)


def body(left_env, right_env, psi, orders, sources, active):
    size = psi.shape[-1]
    terms = sources.shape[0]
    sectors = lax.axis_size("sec")
    planes = sectors // PAIR
    bonds = lax.axis_size("seg")
    half = pltpu.VMEM((size, size // PAIR), psi.dtype)
    sums = pltpu.VMEM((size, size), jnp.float32)
    swap = [(i, i + 1 - PAIR * (i % PAIR)) for i in range(sectors)]
    ring = ring_route(planes)

    def kernel(fn, operands, **kwargs):
        return pl.pallas_call(fn, compiler_params=ROOM, **kwargs)(*operands)

    mine, other = kernel(
        split_kernel,
        (far(orders), far(psi)),
        out_shape=(half, half),
        in_specs=[HBM] * 2,
        out_specs=(VMEM, VMEM),
        scratch_shapes=[
            pltpu.SMEM(orders.shape, orders.dtype),
            pltpu.VMEM(psi.shape, psi.dtype),
            pltpu.SemaphoreType.DMA((2,)),
        ],
    )
    plan = kernel(
        functools.partial(plan_kernel, planes),
        (far(sources), far(active), far(orders)),
        out_shape=pltpu.VMEM((Plan(terms).rows, 128), jnp.int32),
        in_specs=[HBM] * 3,
        out_specs=VMEM,
        scratch_shapes=[pltpu.SMEM(x.shape, x.dtype) for x in (sources, active, orders)]
        + [pltpu.SemaphoreType.DMA((3,))],
    )
    held = [mine, lax.ppermute(other, "sec", swap)]
    left = near(left_env)
    right = near(lax.ppermute(right_env, "seg", [((i + 1) % bonds, i) for i in range(bonds)]))
    while len(held) < sectors:
        held.append(lax.ppermute(held[-PAIR], "sec", ring))
    passed = []
    for slot in range(terms):
        usable = held[: sectors - terms + slot]
        chosen = kernel(
            functools.partial(choose_kernel, Plan(terms).send + slot),
            [near(x) for x in (plan, *usable)],
            out_shape=half,
            in_specs=[VMEM] * (1 + len(usable)),
            out_specs=VMEM,
        )
        passed.append(lax.ppermute(chosen, "sec", swap))
    passed.append(lax.ppermute(held[-1], "sec", swap))

    stages = (
        (range(sectors - 2), range(0)),
        (range(sectors - 2, sectors - 1), range(terms - 2)),
        (range(sectors - 1, sectors), range(terms - 2, terms)),
        (range(0), range(terms, terms + 1)),
    )
    total = []
    for i, (owned, slotted) in enumerate(stages):
        final = i == len(stages) - 1
        operands = [plan, left, right, *(held[j] for j in owned), *(passed[j] for j in slotted), *total]
        total = [
            kernel(
                functools.partial(apply_kernel, terms, owned, slotted, i == 0, final),
                [near(x) for x in operands],
                out_shape=jax.ShapeDtypeStruct(psi.shape, psi.dtype) if final else sums,
                in_specs=[VMEM] * len(operands),
                out_specs=VMEM,
                scratch_shapes=[half] + [sums] * final,
            )
        ]
    return total[0]


def solution(mesh):
    placed = (
        P("seg", "sec", None, None, None),
        P("seg", "sec", None, None, None),
        P("seg", "sec", None, None),
        P("seg", "sec", None),
        P(),
        P("seg", "sec", None),
    )

    def program(*args):
        step = jax.shard_map(body, mesh=mesh, in_specs=placed, out_specs=P("seg", "sec", None, None), check_vma=False)
        return step(*args)

    return program
```

time: 103 us -> 59.5 us (0.58)
  the two profiles are of different devices: /device:TPU:0 before, /device:TPU:12 now
where the time goes in v1:
time: 59.5 us; the launch traced here: 59.3 us
  waiting for transfers between devices  24.3 us (41%)
  starting transfers between devices  24.2 us (41%)
  Pallas kernels  10.7 us (18%)
    ppermute x6, starting transfers between devices, body(): held.append(lax.ppermute(held[-PAIR], 'sec', ring))  17.4 us
    pallas_call x9, Pallas kernels, kernel(): return pl.pallas_call(fn, compiler_params=ROOM, **kwargs)(*operands)  10.7 us
    ppermute x6, waiting for transfers between devices, body(): held.append(lax.ppermute(held[-PAIR], 'sec', ring))  10.2 us
    ppermute x3, waiting for transfers between devices, body(): passed.append(lax.ppermute(chosen, 'sec', swap))  9.34 us
    ppermute x1, waiting for transfers between devices, body(): held = [mine, lax.ppermute(other, 'sec', swap)]  4.64 us
    ppermute x3, starting transfers between devices, body(): passed.append(lax.ppermute(chosen, 'sec', swap))  3.71 us
    ppermute x1, starting transfers between devices, body(): held = [mine, lax.ppermute(other, 'sec', swap)]  1.56 us
    ppermute x1, starting transfers between devices, body(): passed.append(lax.ppermute(held[-1], 'sec', swap))  1.49 us
  transfers between devices with their start and end apart: 12, of which 9 were waited for; matrix products, arithmetic and copies ran while one was open for 0% of the time, Pallas kernels for 15%

profile of v1, /device:TPU:12, one launch (start us, length us, event | category | flops | bytes accessed | tf_op | source)
XLA Modules:
  0.0 59.3 jit_solution(15480337864877262992)
XLA Ops:
  0.0 0.0 collective-permute-start
  0.0 1.3 %shard_map.65 = (bf16[512,256]{1,0:T(8,128)(2,1)S(1)}, bf16[512,256]{1,0:T(8,128)(2,1)S(1)}) custom-call(s32[1,1,2]{2,1,0:T(1,128)} %orders_hbm.3, bf16[1,1,512,512]{3,2,1,0:T(8,128)(2,1)} %psi_hbm.1), custom_call_target="tpu_custom_call" | custom-call | tf_op jit(solution)/shard_map/pallas_call | solution.py:182
  1.3 1.6 %collective-permute-start.1 = (bf16[512,256]{1,0:T(8,128)(2,1)S(1)}, bf16[512,256]{1,0:T(8,128)(2,1)S(1)}, u32[]{:S(2)}, u32[]{:S(2)}) collective-permute-start(bf16[512,256]{1,0:T(8,128)(2,1)S(1)} %get-tuple-element.7), channel_id=1, source_target_pairs={{0,1},{1,0},{2,3},{3,2},{4,5},{5,4},{6,7},{7,6},{8,9},{9,8},{10,11... | collective-permute-start | bytes 786440 | tf_op jit(solution)/shard_map/ppermute | solution.py:205
  2.9 2.6 %collective-permute-start.6 = (bf16[512,256]{1,0:T(8,128)(2,1)S(1)}, bf16[512,256]{1,0:T(8,128)(2,1)S(1)}, u32[]{:S(2)}, u32[]{:S(2)}) collective-permute-start(bf16[512,256]{1,0:T(8,128)(2,1)S(1)} %get-tuple-element.8.refs_0_), channel_id=1, source_target_pairs={{0,2},{1,3},{2,6},{3,7},{6,4},{7,5},{4,0},{5,1},{8,10},{9,11},{10,... | collective-permute-start | bytes 786440 | tf_op jit(solution)/shard_map/ppermute | solution.py:209
  5.4 4.6 %collective-permute-done.1.refs_1_ = bf16[512,256]{1,0:T(8,128)(2,1)S(1)} collective-permute-done((bf16[512,256]{1,0:T(8,128)(2,1)S(1)}, bf16[512,256]{1,0:T(8,128)(2,1)S(1)}, u32[]{:S(2)}, u32[]{:S(2)}) %collective-permute-start.1) | collective-permute-done | bytes 262176 | tf_op jit(solution)/shard_map/ppermute | solution.py:205
  10.1 2.6 %collective-permute-start.2 = (bf16[512,256]{1,0:T(8,128)(2,1)S(1)}, bf16[512,256]{1,0:T(8,128)(2,1)S(1)}, u32[]{:S(2)}, u32[]{:S(2)}) collective-permute-start(bf16[512,256]{1,0:T(8,128)(2,1)S(1)} %collective-permute-done.1.refs_1_), channel_id=1, source_target_pairs={{0,2},{1,3},{2,6},{3,7},{6,4},{7,5},{4,0},{5,1},{8,10},{9,11},{10,... | collective-permute-start | bytes 786440 | tf_op jit(solution)/shard_map/ppermute | solution.py:209
  12.7 2.1 %collective-permute-start.7 = (bf16[512,256]{1,0:T(8,128)(2,1)S(1)}, bf16[512,256]{1,0:T(8,128)(2,1)S(1)}, u32[]{:S(2)}, u32[]{:S(2)}) collective-permute-start(bf16[512,256]{1,0:T(8,128)(2,1)S(1)} %collective-permute-done.6.refs_2_), channel_id=1, source_target_pairs={{0,2},{1,3},{2,6},{3,7},{6,4},{7,5},{4,0},{5,1},{8,10},{9,11},{10,... | collective-permute-start | bytes 786440 | tf_op jit(solution)/shard_map/ppermute | solution.py:209
  14.8 4.6 %collective-permute-done.2.refs_3_ = bf16[512,256]{1,0:T(8,128)(2,1)S(1)} collective-permute-done((bf16[512,256]{1,0:T(8,128)(2,1)S(1)}, bf16[512,256]{1,0:T(8,128)(2,1)S(1)}, u32[]{:S(2)}, u32[]{:S(2)}) %collective-permute-start.2) | collective-permute-done | bytes 262176 | tf_op jit(solution)/shard_map/ppermute | solution.py:209
  19.4 3.4 %collective-permute-start.3 = (bf16[512,256]{1,0:T(8,128)(2,1)S(1)}, bf16[512,256]{1,0:T(8,128)(2,1)S(1)}, u32[]{:S(2)}, u32[]{:S(2)}) collective-permute-start(bf16[512,256]{1,0:T(8,128)(2,1)S(1)} %collective-permute-done.2.refs_3_), channel_id=1, source_target_pairs={{0,2},{1,3},{2,6},{3,7},{6,4},{7,5},{4,0},{5,1},{8,10},{9,11},{10,... | collective-permute-start | bytes 786440 | tf_op jit(solution)/shard_map/ppermute | solution.py:209
  22.7 2.2 %collective-permute-done.7.refs_4_ = bf16[512,256]{1,0:T(8,128)(2,1)S(1)} collective-permute-done((bf16[512,256]{1,0:T(8,128)(2,1)S(1)}, bf16[512,256]{1,0:T(8,128)(2,1)S(1)}, u32[]{:S(2)}, u32[]{:S(2)}) %collective-permute-start.7) | collective-permute-done | bytes 262176 | tf_op jit(solution)/shard_map/ppermute | solution.py:209
  25.0 3.4 %collective-permute-start.9 = (bf16[512,256]{1,0:T(8,128)(2,1)S(1)}, bf16[512,256]{1,0:T(8,128)(2,1)S(1)}, u32[]{:S(2)}, u32[]{:S(2)}) collective-permute-start(bf16[512,256]{1,0:T(8,128)(2,1)S(1)} %collective-permute-done.7.refs_4_), channel_id=1, source_target_pairs={{0,2},{1,3},{2,6},{3,7},{6,4},{7,5},{4,0},{5,1},{8,10},{9,11},{10,... | collective-permute-start | bytes 786440 | tf_op jit(solution)/shard_map/ppermute | solution.py:209
  28.4 2.2 %collective-permute-done.3.refs_5_ = bf16[512,256]{1,0:T(8,128)(2,1)S(1)} collective-permute-done((bf16[512,256]{1,0:T(8,128)(2,1)S(1)}, bf16[512,256]{1,0:T(8,128)(2,1)S(1)}, u32[]{:S(2)}, u32[]{:S(2)}) %collective-permute-start.3) | collective-permute-done | bytes 262176 | tf_op jit(solution)/shard_map/ppermute | solution.py:209
  30.6 3.4 %collective-permute-start.4 = (bf16[512,256]{1,0:T(8,128)(2,1)S(1)}, bf16[512,256]{1,0:T(8,128)(2,1)S(1)}, u32[]{:S(2)}, u32[]{:S(2)}) collective-permute-start(bf16[512,256]{1,0:T(8,128)(2,1)S(1)} %collective-permute-done.3.refs_5_), channel_id=1, source_target_pairs={{0,2},{1,3},{2,6},{3,7},{6,4},{7,5},{4,0},{5,1},{8,10},{9,11},{10,... | collective-permute-start | bytes 786440 | tf_op jit(solution)/shard_map/ppermute | solution.py:209
  34.0 1.0 %shard_map.64.plan_ref = s32[14,128]{1,0:T(8,128)S(1)} custom-call(s32[3,8]{1,0:T(4,128)} %sources_hbm.1, s32[1,1,3]{2,1,0:T(1,128)} %active_hbm.1, s32[1,1,2]{2,1,0:T(1,128)} %orders_hbm.3), custom_call_target="tpu_custom_call" | custom-call | tf_op jit(solution)/shard_map/pallas_call | solution.py:182
  34.9 0.2 shard_map.68
  35.2 0.0 copy-start
  35.2 1.6 %collective-permute-start.11 = (bf16[512,256]{1,0:T(8,128)(2,1)S(1)}, bf16[512,256]{1,0:T(8,128)(2,1)S(1)}, u32[]{:S(2)}, u32[]{:S(2)}) collective-permute-start(bf16[512,256]{1,0:T(8,128)(2,1)S(1)} %shard_map.68), channel_id=1, source_target_pairs={{0,1},{1,0},{2,3},{3,2},{4,5},{5,4},{6,7},{7,6},{8,9},{9,8},{10,11... | collective-permute-start | bytes 786440 | tf_op jit(solution)/shard_map/ppermute | solution.py:220
  36.8 0.2 shard_map.66
  37.0 0.6 %collective-permute-start.8 = (bf16[512,256]{1,0:T(8,128)(2,1)S(1)}, bf16[512,256]{1,0:T(8,128)(2,1)S(1)}, u32[]{:S(2)}, u32[]{:S(2)}) collective-permute-start(bf16[512,256]{1,0:T(8,128)(2,1)S(1)} %shard_map.66), channel_id=1, source_target_pairs={{0,1},{1,0},{2,3},{3,2},{4,5},{5,4},{6,7},{7,6},{8,9},{9,8},{10,11... | collective-permute-start | bytes 786440 | tf_op jit(solution)/shard_map/ppermute | solution.py:220
  37.6 0.0 collective-permute-done.9.refs_6_.refs_0_
  37.6 0.2 shard_map.67
  37.9 1.6 %collective-permute-start.10 = (bf16[512,256]{1,0:T(8,128)(2,1)S(1)}, bf16[512,256]{1,0:T(8,128)(2,1)S(1)}, u32[]{:S(2)}, u32[]{:S(2)}) collective-permute-start(bf16[512,256]{1,0:T(8,128)(2,1)S(1)} %shard_map.67), channel_id=1, source_target_pairs={{0,1},{1,0},{2,3},{3,2},{4,5},{5,4},{6,7},{7,6},{8,9},{9,8},{10,11... | collective-permute-start | bytes 786440 | tf_op jit(solution)/shard_map/ppermute | solution.py:220
  39.4 1.1 %collective-permute-done.4.refs_0_ = bf16[512,256]{1,0:T(8,128)(2,1)S(1)} collective-permute-done((bf16[512,256]{1,0:T(8,128)(2,1)S(1)}, bf16[512,256]{1,0:T(8,128)(2,1)S(1)}, u32[]{:S(2)}, u32[]{:S(2)}) %collective-permute-start.4) | collective-permute-done | bytes 262176 | tf_op jit(solution)/shard_map/ppermute | solution.py:209
  40.5 1.5 %collective-permute-start.5 = (bf16[512,256]{1,0:T(8,128)(2,1)S(1)}, bf16[512,256]{1,0:T(8,128)(2,1)S(1)}, u32[]{:S(2)}, u32[]{:S(2)}) collective-permute-start(bf16[512,256]{1,0:T(8,128)(2,1)S(1)} %collective-permute-done.4.refs_0_), channel_id=1, source_target_pairs={{0,1},{1,0},{2,3},{3,2},{4,5},{5,4},{6,7},{7,6},{8,9},{9,8},{10,11... | collective-permute-start | bytes 786440 | tf_op jit(solution)/shard_map/ppermute | solution.py:221
  42.0 2.1 %shard_map.69.refs_2_ = f32[512,512]{1,0:T(8,128)S(1)} custom-call(s32[14,128]{1,0:T(8,128)S(1)} %shard_map.64.plan_ref, bf16[1,1,3,512,512]{4,3,2,1,0:T(8,128)(2,1)S(1)} %copy-done, bf16[1,1,3,512,512]{4,3,2,1,0:T(8,128)(2,1)S(1)} %collective-permute-done.right_ref, bf16[512,256]{1,0:T(8,128)(2,1)S(1)} %get-tuple-element.8.refs_0_, ...), custom_call_target="tpu_custom_call" | custom-call | tf_op jit(solution)/shard_map/pallas_call | solution.py:182
  44.1 0.3 collective-permute-done.11.refs_1_
  44.4 1.3 %shard_map.70.refs_3_ = f32[512,512]{1,0:T(8,128)S(1)} custom-call(s32[14,128]{1,0:T(8,128)S(1)} %shard_map.64.plan_ref, bf16[1,1,3,512,512]{4,3,2,1,0:T(8,128)(2,1)S(1)} %copy-done, bf16[1,1,3,512,512]{4,3,2,1,0:T(8,128)(2,1)S(1)} %collective-permute-done.right_ref, bf16[512,256]{1,0:T(8,128)(2,1)S(1)} %collective-permute-done.9.refs_6_.refs_0_, ...), custom_call_target="tpu_custom_call" | custom-call | tf_op jit(solution)/shard_map/pallas_call | solution.py:182
  45.7 4.4 %collective-permute-done.8.refs_1_ = bf16[512,256]{1,0:T(8,128)(2,1)S(1)} collective-permute-done((bf16[512,256]{1,0:T(8,128)(2,1)S(1)}, bf16[512,256]{1,0:T(8,128)(2,1)S(1)}, u32[]{:S(2)}, u32[]{:S(2)}) %collective-permute-start.8) | collective-permute-done | bytes 262176 | tf_op jit(solution)/shard_map/ppermute | solution.py:220
  50.1 4.7 %collective-permute-done.10.refs_2_ = bf16[512,256]{1,0:T(8,128)(2,1)S(1)} collective-permute-done((bf16[512,256]{1,0:T(8,128)(2,1)S(1)}, bf16[512,256]{1,0:T(8,128)(2,1)S(1)}, u32[]{:S(2)}, u32[]{:S(2)}) %collective-permute-start.10) | collective-permute-done | bytes 262176 | tf_op jit(solution)/shard_map/ppermute | solution.py:220
  54.7 2.6 %shard_map.71.refs_1_ = f32[512,512]{1,0:T(8,128)S(1)} custom-call(s32[14,128]{1,0:T(8,128)S(1)} %shard_map.64.plan_ref, bf16[1,1,3,512,512]{4,3,2,1,0:T(8,128)(2,1)S(1)} %copy-done, bf16[1,1,3,512,512]{4,3,2,1,0:T(8,128)(2,1)S(1)} %collective-permute-done.right_ref, bf16[512,256]{1,0:T(8,128)(2,1)S(1)} %collective-permute-done.4.refs_0_, ...), custom_call_target="tpu_custom_call" | custom-call | tf_op jit(solution)/shard_map/pallas_call | solution.py:182
  57.4 0.2 collective-permute-done.5.refs_0_
  57.5 1.8 %shard_map.72 = bf16[1,1,512,512]{3,2,1,0:T(8,128)(2,1)} custom-call(s32[14,128]{1,0:T(8,128)S(1)} %shard_map.64.plan_ref, bf16[1,1,3,512,512]{4,3,2,1,0:T(8,128)(2,1)S(1)} %copy-done, bf16[1,1,3,512,512]{4,3,2,1,0:T(8,128)(2,1)S(1)} %collective-permute-done.right_ref, bf16[512,256]{1,0:T(8,128)(2,1)S(1)} %collective-permute-done.5.refs_0_, ...), custom_call_target="tpu_custom_call" | custom-call | tf_op jit(solution)/shard_map/pallas_call | solution.py:182
  (3 shorter events, 0.0 us)
Async XLA Ops:
  0.0 42.0 %collective-permute-start = (bf16[1,1,3,512,512]{4,3,2,1,0:T(8,128)(2,1)}, bf16[1,1,3,512,512]{4,3,2,1,0:T(8,128)(2,1)S(1)}, u32[]{:S(2)}, u32[]{:S(2)}) collective-permute-start(bf16[1,1,3,512,512]{4,3,2,1,0:T(8,128)(2,1)} %param.7), channel_id=1, source_target_pairs={{8,0},{16,8},{24,16},{0,24},{9,1},{17,9},{25,17},{1,25},{10,2},{18... | collective-permute-start | bytes 4718600 | tf_op jit(solution)/shard_map/ppermute | solution.py:207
  1.3 8.8 %collective-permute-start.1 = (bf16[512,256]{1,0:T(8,128)(2,1)S(1)}, bf16[512,256]{1,0:T(8,128)(2,1)S(1)}, u32[]{:S(2)}, u32[]{:S(2)}) collective-permute-start(bf16[512,256]{1,0:T(8,128)(2,1)S(1)} %get-tuple-element.7), channel_id=1, source_target_pairs={{0,1},{1,0},{2,3},{3,2},{4,5},{5,4},{6,7},{7,6},{8,9},{9,8},{10,11... | collective-permute-start | bytes 786440 | tf_op jit(solution)/shard_map/ppermute | solution.py:205
  2.9 9.8 %collective-permute-start.6 = (bf16[512,256]{1,0:T(8,128)(2,1)S(1)}, bf16[512,256]{1,0:T(8,128)(2,1)S(1)}, u32[]{:S(2)}, u32[]{:S(2)}) collective-permute-start(bf16[512,256]{1,0:T(8,128)(2,1)S(1)} %get-tuple-element.8.refs_0_), channel_id=1, source_target_pairs={{0,2},{1,3},{2,6},{3,7},{6,4},{7,5},{4,0},{5,1},{8,10},{9,11},{10,... | collective-permute-start | bytes 786440 | tf_op jit(solution)/shard_map/ppermute | solution.py:209
  10.1 9.3 %collective-permute-start.2 = (bf16[512,256]{1,0:T(8,128)(2,1)S(1)}, bf16[512,256]{1,0:T(8,128)(2,1)S(1)}, u32[]{:S(2)}, u32[]{:S(2)}) collective-permute-start(bf16[512,256]{1,0:T(8,128)(2,1)S(1)} %collective-permute-done.1.refs_1_), channel_id=1, source_target_pairs={{0,2},{1,3},{2,6},{3,7},{6,4},{7,5},{4,0},{5,1},{8,10},{9,11},{10,... | collective-permute-start | bytes 786440 | tf_op jit(solution)/shard_map/ppermute | solution.py:209
  12.7 12.3 %collective-permute-start.7 = (bf16[512,256]{1,0:T(8,128)(2,1)S(1)}, bf16[512,256]{1,0:T(8,128)(2,1)S(1)}, u32[]{:S(2)}, u32[]{:S(2)}) collective-permute-start(bf16[512,256]{1,0:T(8,128)(2,1)S(1)} %collective-permute-done.6.refs_2_), channel_id=1, source_target_pairs={{0,2},{1,3},{2,6},{3,7},{6,4},{7,5},{4,0},{5,1},{8,10},{9,11},{10,... | collective-permute-start | bytes 786440 | tf_op jit(solution)/shard_map/ppermute | solution.py:209
  19.4 11.2 %collective-permute-start.3 = (bf16[512,256]{1,0:T(8,128)(2,1)S(1)}, bf16[512,256]{1,0:T(8,128)(2,1)S(1)}, u32[]{:S(2)}, u32[]{:S(2)}) collective-permute-start(bf16[512,256]{1,0:T(8,128)(2,1)S(1)} %collective-permute-done.2.refs_3_), channel_id=1, source_target_pairs={{0,2},{1,3},{2,6},{3,7},{6,4},{7,5},{4,0},{5,1},{8,10},{9,11},{10,... | collective-permute-start | bytes 786440 | tf_op jit(solution)/shard_map/ppermute | solution.py:209
  25.0 12.6 %collective-permute-start.9 = (bf16[512,256]{1,0:T(8,128)(2,1)S(1)}, bf16[512,256]{1,0:T(8,128)(2,1)S(1)}, u32[]{:S(2)}, u32[]{:S(2)}) collective-permute-start(bf16[512,256]{1,0:T(8,128)(2,1)S(1)} %collective-permute-done.7.refs_4_), channel_id=1, source_target_pairs={{0,2},{1,3},{2,6},{3,7},{6,4},{7,5},{4,0},{5,1},{8,10},{9,11},{10,... | collective-permute-start | bytes 786440 | tf_op jit(solution)/shard_map/ppermute | solution.py:209
  30.6 9.9 %collective-permute-start.4 = (bf16[512,256]{1,0:T(8,128)(2,1)S(1)}, bf16[512,256]{1,0:T(8,128)(2,1)S(1)}, u32[]{:S(2)}, u32[]{:S(2)}) collective-permute-start(bf16[512,256]{1,0:T(8,128)(2,1)S(1)} %collective-permute-done.3.refs_5_), channel_id=1, source_target_pairs={{0,2},{1,3},{2,6},{3,7},{6,4},{7,5},{4,0},{5,1},{8,10},{9,11},{10,... | collective-permute-start | bytes 786440 | tf_op jit(solution)/shard_map/ppermute | solution.py:209
  35.2 6.8 %copy-start = (bf16[1,1,3,512,512]{4,3,2,1,0:T(8,128)(2,1)S(1)}, bf16[1,1,3,512,512]{4,3,2,1,0:T(8,128)(2,1)}, u32[]{:S(2)}) copy-start(bf16[1,1,3,512,512]{4,3,2,1,0:T(8,128)(2,1)} %left_ref.7) | copy-start | bytes 4718596
  35.2 9.2 %collective-permute-start.11 = (bf16[512,256]{1,0:T(8,128)(2,1)S(1)}, bf16[512,256]{1,0:T(8,128)(2,1)S(1)}, u32[]{:S(2)}, u32[]{:S(2)}) collective-permute-start(bf16[512,256]{1,0:T(8,128)(2,1)S(1)} %shard_map.68), channel_id=1, source_target_pairs={{0,1},{1,0},{2,3},{3,2},{4,5},{5,4},{6,7},{7,6},{8,9},{9,8},{10,11... | collective-permute-start | bytes 786440 | tf_op jit(solution)/shard_map/ppermute | solution.py:220
  37.0 13.1 %collective-permute-start.8 = (bf16[512,256]{1,0:T(8,128)(2,1)S(1)}, bf16[512,256]{1,0:T(8,128)(2,1)S(1)}, u32[]{:S(2)}, u32[]{:S(2)}) collective-permute-start(bf16[512,256]{1,0:T(8,128)(2,1)S(1)} %shard_map.66), channel_id=1, source_target_pairs={{0,1},{1,0},{2,3},{3,2},{4,5},{5,4},{6,7},{7,6},{8,9},{9,8},{10,11... | collective-permute-start | bytes 786440 | tf_op jit(solution)/shard_map/ppermute | solution.py:220
  37.9 16.9 %collective-permute-start.10 = (bf16[512,256]{1,0:T(8,128)(2,1)S(1)}, bf16[512,256]{1,0:T(8,128)(2,1)S(1)}, u32[]{:S(2)}, u32[]{:S(2)}) collective-permute-start(bf16[512,256]{1,0:T(8,128)(2,1)S(1)} %shard_map.67), channel_id=1, source_target_pairs={{0,1},{1,0},{2,3},{3,2},{4,5},{5,4},{6,7},{7,6},{8,9},{9,8},{10,11... | collective-permute-start | bytes 786440 | tf_op jit(solution)/shard_map/ppermute | solution.py:220
  40.5 17.0 %collective-permute-start.5 = (bf16[512,256]{1,0:T(8,128)(2,1)S(1)}, bf16[512,256]{1,0:T(8,128)(2,1)S(1)}, u32[]{:S(2)}, u32[]{:S(2)}) collective-permute-start(bf16[512,256]{1,0:T(8,128)(2,1)S(1)} %collective-permute-done.4.refs_0_), channel_id=1, source_target_pairs={{0,1},{1,0},{2,3},{3,2},{4,5},{5,4},{6,7},{7,6},{8,9},{9,8},{10,11... | collective-permute-start | bytes 786440 | tf_op jit(solution)/shard_map/ppermute | solution.py:221
